TPU v7x, 32 devices: a whole 2x2x4 slice. The times are simulated.
32 devices in a mesh: replica: 8 (over z, x), shard: 4 (over y, core).
Axes of the slice: x: 2, y: 2, z: 4, core: 2. Of those that a mesh axis runs over, the one named last changes fastest.
Arguments:
- hidden_in: bfloat16 [4096, 768], P(('replica', 'shard')), may hold values from -6 to 6
- out_cot: bfloat16 [4096, 768], P(('replica', 'shard')), may hold values from -6 to 6
- pre_gain: float32 [2, 768], replicated, may hold values from 0.5 to 1.5
- in_weight: bfloat16 [2, 768, 3352], P(None, 'shard'), may hold values from -0.21875 to 0.21875
- conv_weight: float32 [2, 4, 1792], replicated, may hold values from -2.4 to 2.4
- conv_bias: float32 [2, 1792], replicated, may hold values from -0.5 to 0.5
- dt_bias: float32 [2, 24], replicated, may hold values from -6 to -2
- a_log: float32 [2, 24], replicated, may hold values from -1.2 to 2
- skip: float32 [2, 24], replicated, may hold values from 0.5 to 1.5
- norm_gain: float32 [2, 1536], replicated, may hold values from 0.5 to 1.5
- out_weight: bfloat16 [2, 1536, 768], P(None, 'shard'), may hold values from -0.15625 to 0.15625
Outputs:
- block_out: bfloat16 [4096, 768], P(('replica', 'shard'))
- grad_in: float32 [4096, 768], P(('replica', 'shard'))
- grad_pre_gain: float32 [2, 768], replicated
- grad_in_weight: float32 [2, 768, 3352], P(None, 'shard')
- grad_conv_weight: float32 [2, 4, 1792], replicated
- grad_conv_bias: float32 [2, 1792], replicated
- grad_dt_bias: float32 [2, 24], replicated
- grad_a_log: float32 [2, 24], replicated
- grad_skip: float32 [2, 24], replicated
- grad_norm_gain: float32 [2, 1536], replicated
- grad_out_weight: float32 [2, 1536, 768], P(None, 'shard')
All inputs are finite; a program needn't handle non-finite values.
Results may differ from a plain program's by a relative error of at most 0.014.
Values may be sent and summed in bfloat16 or wider, within the bound.
A program may use at most 192 MiB of HBM per device.

v0:
```python
import jax
import jax.numpy as jnp
from jax import lax
from jax.sharding import PartitionSpec as P

DI = 1536
HEADS = 24
HEAD_DIM = 64
STATE = 128
CONV = 4
SPAN = 128
EPS = 1e-05
EXACT = lax.Precision.HIGHEST


def from_behind(value, axis, steps):
    count = lax.axis_size(axis)
    initial, last = (max(0, -steps), min(count, count - steps))
    return lax.ppermute(value, axis, [(source, source + steps) for source in range(initial, last)])


def carried_in(array, axis, combine, identity):
    length, position = (lax.axis_size(axis), lax.axis_index(axis))
    everything = jax.tree.map(lambda part: lax.all_gather(part, axis), array)
    start = jax.tree.map(
        lambda part, zero: jnp.broadcast_to(jnp.asarray(zero, part.dtype), part.shape),
        array,
        identity,
    )

    def turn(k, before):
        reached = k < position
        new = combine(before, jax.tree.map(lambda part: part[k], everything))
        return jax.tree.map(lambda a, b: jnp.where(reached, a, b), new, before)

    return lax.fori_loop(0, length, turn, start)


def entering_2(array, axis, join, neutral):
    count = lax.axis_size(axis)
    place = lax.axis_index(axis)
    ahead = count - 1 - place
    gathered = jax.tree.map(
        lambda a, kind: lax.all_gather(a.astype(kind), axis),
        array,
        jax.tree.map(lambda a: jnp.bfloat16 if a.dtype == jnp.float32 else a.dtype, array),
    )
    state = jax.tree.map(lambda a, e: jnp.zeros_like(a) + jnp.asarray(e, a.dtype), array, neutral)

    def one(turn, state):
        source = count - 1 - turn
        return join(
            state,
            jax.tree.map(
                lambda a, own: lax.dynamic_index_in_dim(a, source, 0, False).astype(own.dtype),
                gathered,
                array,
            ),
        )

    return lax.fori_loop(0, ahead, one, state)


def rms_scale(residual, gain):
    mean_sq = jnp.mean(residual * residual, axis=-1, keepdims=True)
    return residual * lax.rsqrt(mean_sq + EPS) * gain


def compose(earlier, later):
    return (earlier[0] * later[0], later[1] + later[0][..., None, None] * earlier[1])


def unpack(projected, rim_rows):
    channels = DI + 2 * STATE
    xbc_ext = jnp.concatenate([rim_rows, projected[:, DI : DI + channels]], axis=0).astype(
        jnp.float32
    )
    return (
        xbc_ext,
        projected[:, DI + channels :].astype(jnp.float32),
        projected[:, :DI].astype(jnp.float32),
    )


def prepare(xbc_ext, dt_raw, conv_w, conv_b, dt_shift, a_log):
    length = xbc_ext.shape[0] - (CONV - 1)
    conv_out = conv_b + conv_w[0] * xbc_ext[0:length]
    for offset in range(1, CONV):
        conv_out = conv_out + conv_w[offset] * xbc_ext[offset : offset + length]
    activated = jax.nn.silu(conv_out)
    blocks = length // SPAN
    x_heads = activated[:, :DI].reshape(blocks, SPAN, HEADS, HEAD_DIM)
    write_proj = activated[:, DI : DI + STATE].reshape(blocks, SPAN, STATE)
    read_proj = activated[:, DI + STATE :].reshape(blocks, SPAN, STATE)
    step_size = jax.nn.softplus(dt_raw + dt_shift)
    decay_rate = -jnp.exp(a_log)
    log_decay = jnp.cumsum((step_size * decay_rate).reshape(blocks, SPAN, HEADS), axis=1)
    return (x_heads, write_proj, read_proj, step_size.reshape(blocks, SPAN, HEADS), log_decay)


def states(x_heads, write_proj, step_size, log_decay):
    to_end = jnp.exp(log_decay[:, -1:, :] - log_decay) * step_size
    weighted = x_heads * to_end[..., None]
    span_sum = jnp.einsum("cshp,csn->chpn", weighted, write_proj, precision=EXACT)
    span_decay = jnp.exp(log_decay[:, -1, :])

    def fold(carry, item):
        return (compose(carry, item), None)

    begin = (jnp.ones_like(span_decay[0]), jnp.zeros_like(span_sum[0]))
    total, _ = lax.scan(fold, begin, (span_decay, span_sum))
    return (total[1], total[0], span_sum, span_decay)


def outputs(
    x_heads,
    write_proj,
    read_proj,
    step_size,
    log_decay,
    span_sum,
    span_decay,
    entering,
    zgate,
    skip_gain,
    norm_gain,
):

    def advance(carry, item):
        return (item[1] + item[0][:, None, None] * carry, carry)

    _, before = lax.scan(advance, entering, (span_decay, span_sum))
    scores = jnp.einsum("ctn,csn->cts", read_proj, write_proj, precision=EXACT)
    decay_heads = jnp.swapaxes(log_decay, 1, 2)
    step_heads = jnp.swapaxes(step_size, 1, 2)
    gap = decay_heads[:, :, :, None] - decay_heads[:, :, None, :]
    causal = (jnp.arange(SPAN)[:, None] >= jnp.arange(SPAN)[None, :])[None, None, :, :]
    mixing = (
        jnp.exp(jnp.where(causal, gap, -jnp.inf))
        * scores[:, None, :, :]
        * step_heads[:, :, None, :]
    )
    inside = jnp.einsum("chts,cshp->cthp", mixing, x_heads, precision=EXACT)
    carried = (
        jnp.einsum("ctn,chpn->cthp", read_proj, before, precision=EXACT)
        * jnp.exp(log_decay)[..., None]
    )
    mixed = inside + carried + skip_gain[:, None] * x_heads
    flat_rows = mixed.reshape(-1, HEADS * HEAD_DIM)
    return rms_scale(flat_rows * jax.nn.silu(zgate), norm_gain)


def inner_rows(left, right):
    return lax.dot_general(
        left, right, (((0,), (0,)), ((), ())), preferred_element_type=jnp.float32
    )


def outer_cols(left, right):
    return lax.dot_general(
        left, right, (((1,), (1,)), ((), ())), preferred_element_type=jnp.float32
    )


def shards(
    hidden_in,
    out_cot,
    pre_gain,
    in_weight,
    conv_weight,
    conv_bias,
    dt_bias,
    a_log,
    skip,
    norm_gain,
    out_weight,
):
    layer_count = in_weight.shape[0]
    rim_width = CONV - 1
    channels = DI + 2 * STATE
    residual = hidden_in.astype(jnp.float32)
    token_rows = residual.shape[0]
    in_rows = in_weight.shape[1]
    out_rows = out_weight.shape[1]
    saved = []
    for section_no in range(layer_count):
        normed = rms_scale(residual, pre_gain[section_no]).astype(jnp.bfloat16)

        def add_in(total, piece, start, normed=normed):
            return jnp.dot(normed, piece, preferred_element_type=jnp.float32)

        projected = add_in(
            jnp.zeros((token_rows, in_weight.shape[2]), jnp.float32),
            lax.all_gather(in_weight[section_no], "shard", axis=0, tiled=True),
            jnp.int32(0),
        )
        projected = projected.astype(jnp.bfloat16)
        rim_rows = from_behind(projected[token_rows - rim_width :, DI : DI + channels], "shard", 1)
        xbc_ext, dt_raw, zgate = unpack(projected, rim_rows)
        pieces = prepare(
            xbc_ext,
            dt_raw,
            conv_weight[section_no],
            conv_bias[section_no],
            dt_bias[section_no],
            a_log[section_no],
        )
        st_tot, dec_tot, span_sum, span_decay = states(pieces[0], pieces[1], pieces[3], pieces[4])
        entering = carried_in(
            (dec_tot, st_tot), "shard", compose, (jnp.ones_like(dec_tot), jnp.zeros_like(st_tot))
        )[1]
        gated_out = outputs(
            pieces[0],
            pieces[1],
            pieces[2],
            pieces[3],
            pieces[4],
            span_sum,
            span_decay,
            entering,
            zgate,
            skip[section_no],
            norm_gain[section_no],
        ).astype(jnp.bfloat16)

        def add_out(total, piece, start, gated_out=gated_out):
            return jnp.dot(gated_out, piece, preferred_element_type=jnp.float32)

        mixed = add_out(
            jnp.zeros((token_rows, out_weight.shape[2]), jnp.float32),
            lax.all_gather(out_weight[section_no], "shard", axis=0, tiled=True),
            jnp.int32(0),
        )
        saved.append((residual, normed, projected, rim_rows, entering, gated_out))
        residual = residual + mixed
    block_out = residual.astype(jnp.bfloat16)
    cotangent = out_cot.astype(jnp.float32)
    big_in = [None] * layer_count
    big_out = [None] * layer_count
    small = [None] * layer_count
    for section_no in reversed(range(layer_count)):
        residual_in, normed, projected, rim_rows, entering, gated_out = saved[section_no]
        cot_bf = cotangent.astype(jnp.bfloat16)

        def out_term(start, count, gated_out=gated_out, cot_bf=cot_bf):
            return inner_rows(gated_out, cot_bf)

        grad_out_w = lax.psum_scatter(
            out_term(jnp.int32(0), lax.axis_size("shard") * out_rows).astype(jnp.bfloat16),
            "shard",
            scatter_dimension=0,
            tiled=True,
        ).astype(jnp.float32)

        def back_out(piece, start, cot_bf=cot_bf):
            return outer_cols(cot_bf, piece)

        grad_gated = back_out(
            lax.all_gather(out_weight[section_no], "shard", axis=0, tiled=True), jnp.int32(0)
        )
        xbc_ext, dt_raw, zgate = unpack(projected, rim_rows)
        pieces, prep_back = jax.vjp(
            prepare,
            xbc_ext,
            dt_raw,
            conv_weight[section_no],
            conv_bias[section_no],
            dt_bias[section_no],
            a_log[section_no],
        )
        stats, state_back = jax.vjp(states, pieces[0], pieces[1], pieces[3], pieces[4])
        _, out_back = jax.vjp(
            outputs,
            pieces[0],
            pieces[1],
            pieces[2],
            pieces[3],
            pieces[4],
            stats[2],
            stats[3],
            entering,
            zgate,
            skip[section_no],
            norm_gain[section_no],
        )
        back_out_g = out_back(grad_gated)
        later_grad = entering_2(
            (stats[1], back_out_g[7]),
            "shard",
            compose,
            (jnp.ones_like(stats[1]), jnp.zeros_like(back_out_g[7])),
        )[1]
        grad_dec = jnp.sum(later_grad * entering, axis=(1, 2))
        from_state = state_back((later_grad, grad_dec, back_out_g[5], back_out_g[6]))
        from_prep = prep_back(
            (
                back_out_g[0] + from_state[0],
                back_out_g[1] + from_state[1],
                back_out_g[2],
                back_out_g[3] + from_state[2],
                back_out_g[4] + from_state[3],
            )
        )
        grad_ext = from_prep[0]
        returned = from_behind(grad_ext[:rim_width], "shard", -1)
        grad_own = grad_ext[rim_width:].at[token_rows - rim_width :].add(returned)
        grad_proj = jnp.concatenate([back_out_g[8], grad_own, from_prep[1]], axis=1).astype(
            jnp.bfloat16
        )

        def in_term(start, count, normed=normed, grad_proj=grad_proj):
            return inner_rows(normed, grad_proj)

        grad_in_w = lax.psum_scatter(
            in_term(jnp.int32(0), lax.axis_size("shard") * in_rows).astype(jnp.bfloat16),
            "shard",
            scatter_dimension=0,
            tiled=True,
        ).astype(jnp.float32)

        def back_in(piece, start, grad_proj=grad_proj):
            return outer_cols(grad_proj, piece)

        grad_normed = back_in(
            lax.all_gather(in_weight[section_no], "shard", axis=0, tiled=True), jnp.int32(0)
        )
        _, norm_back = jax.vjp(rms_scale, residual_in, pre_gain[section_no])
        grad_res, grad_pre = norm_back(grad_normed)
        cotangent = cotangent + grad_res
        small[section_no] = (
            grad_pre,
            from_prep[2],
            from_prep[3],
            from_prep[4],
            from_prep[5],
            back_out_g[9],
            back_out_g[10],
        )
        grad_in_w, grad_out_w = lax.psum((grad_in_w, grad_out_w), "replica")
        big_in[section_no] = grad_in_w
        big_out[section_no] = grad_out_w
    stacked_in = jnp.stack(big_in)
    stacked_out = jnp.stack(big_out)
    columns = [
        jnp.stack([small[number][member] for number in range(layer_count)]) for member in range(7)
    ]
    summed = lax.psum(
        (columns[0], columns[1], columns[2], columns[3], columns[4], columns[5], columns[6]),
        ("replica", "shard"),
    )
    return (
        block_out,
        cotangent,
        summed[0],
        stacked_in,
        summed[1],
        summed[2],
        summed[3],
        summed[4],
        summed[5],
        summed[6],
        stacked_out,
    )


def solution(mesh):
    return jax.shard_map(
        shards,
        mesh=mesh,
        in_specs=(
            P(("replica", "shard"), None),
            P(("replica", "shard"), None),
            P(),
            P(None, "shard", None),
            P(),
            P(),
            P(),
            P(),
            P(),
            P(),
            P(None, "shard", None),
        ),
        out_specs=(
            P(("replica", "shard"), None),
            P(("replica", "shard"), None),
            P(),
            P(None, "shard", None),
            P(),
            P(),
            P(),
            P(),
            P(),
            P(),
            P(None, "shard", None),
        ),
        check_vma=False,
    )
```

profile of v0, /device:TPU:8, one launch (start us, length us, event | category | flops | bytes accessed | tf_op | source)
XLA Modules:
  0.0 944.2 jit_solution(16295703544789042874)
XLA Ops:
  7.3 3.4 fusion.225
  13.9 38.8 %all-gather.21.cloned.1.call-done = bf16[1,768,3352]{2,1,0:T(8,128)(2,1)} async-done(((bf16[1,192,3352]{2,1,0:T(8,128)(2,1)}), bf16[1,768,3352]{2,1,0:T(8,128)(2,1)}) %all-gather.21.cloned.1.call-update) | async-done | bytes 5148688 | tf_op jit(solution)/shard_map/all_gather | solution.py:194
  52.8 3.4 fusion.10
  61.2 2.2 fusion.96
  68.0 2.3 fusion.226
  74.3 5.4 all-gather.2
  81.3 17.1 %all-gather.23.cloned.1.call-done = f32[96,64,128]{2,1,0:T(8,128)} async-done(((f32[24,64,128]{2,1,0:T(8,128)}), f32[96,64,128]{2,1,0:T(8,128)}) %all-gather.23.cloned.1.call-update) | async-done | bytes 3145744 | tf_op jit(solution)/shard_map/all_gather | solution.py:24
  98.4 10.1 %while.40 = (s32[]{:T(128)}, f32[24,64,128]{2,1,0:T(8,128)S(1)}, s32[]{:T(128)}, f32[4,24,64,128]{3,2,1,0:T(8,128)}, f32[4,24]{1,0:T(4,128)}, /*index=5*/s32[]{:T(128)}, s32[]{:T(128)}) while((s32[]{:T(128)}, f32[24,64,128]{2,1,0:T(8,128)S(1)}, s32[]{:T(128)}, f32[4,24,64,128]{3,2,1,0:T(8,128)}, f32[4,24]{1,0:T(4,128)}, ...), condition=%wide.region_3.4_spmd.clone, body=%wide.region_2.3_spmd.clone.sunk | while | flops 786436 | bytes 2359697 | solution.py:36
  109.4 4.1 fusion.69
  117.8 6.2 all-gather.25.cloned.1.call-done
  124.0 2.3 multiply_reduce_fusion.32
  126.4 40.4 %all-gather.27.cloned.1.call-done = bf16[1,768,3352]{2,1,0:T(8,128)(2,1)} async-done(((bf16[1,192,3352]{2,1,0:T(8,128)(2,1)}), bf16[1,768,3352]{2,1,0:T(8,128)(2,1)}) %all-gather.27.cloned.1.call-update) | async-done | bytes 5148688 | tf_op jit(solution)/shard_map/all_gather | solution.py:194
  166.8 3.5 fusion.13
  174.1 2.4 collective-permute-start.1
  182.8 2.6 convolution_add_fusion.2
  192.2 2.4 copy.374
  194.6 5.8 all-gather.6
  200.4 2.3 copy.358
  204.5 10.4 %all-gather.29.cloned.1.call-done = f32[96,64,128]{2,1,0:T(8,128)} async-done(((f32[24,64,128]{2,1,0:T(8,128)}), f32[96,64,128]{2,1,0:T(8,128)}) %all-gather.29.cloned.1.call-update) | async-done | bytes 3145744 | tf_op jit(solution)/shard_map/all_gather | solution.py:24
  214.9 10.2 %while.41 = (s32[]{:T(128)}, f32[24,64,128]{2,1,0:T(8,128)S(1)}, s32[]{:T(128)}, f32[4,24,64,128]{3,2,1,0:T(8,128)}, f32[4,24]{1,0:T(4,128)}, /*index=5*/s32[]{:T(128)}, s32[]{:T(128)}) while((s32[]{:T(128)}, f32[24,64,128]{2,1,0:T(8,128)S(1)}, s32[]{:T(128)}, f32[4,24,64,128]{3,2,1,0:T(8,128)}, f32[4,24]{1,0:T(4,128)}, ...), condition=%wide.region_8.9_spmd.clone, body=%wide.region_7.8_spmd.clone.sunk | while | flops 786436 | bytes 2359697 | solution.py:36
  227.2 4.1 fusion.57
  231.3 2.3 copy.367
  233.6 2.4 multiply_reduce_fusion.28
  237.1 3.3 all-gather.31.cloned.1.call-done
  240.4 3.6 multiply_reduce_fusion.12
  248.0 2.3 copy.375
  250.2 2.7 fusion.72
  254.7 2.3 copy.395
  257.0 5.4 all-gather.9
  263.0 2.3 copy.376
  268.8 5.7 fusion.88
  280.6 2.5 convolution_bitcast_fusion.5
  284.9 6.2 while.38
  291.2 2.7 multiply_reduce_fusion.26
  294.8 2.8 fusion.51
  297.6 2.3 copy.381
  299.9 2.7 fusion.86
  302.6 2.3 multiply_reduce_fusion.7
  319.7 5.1 multiply_reduce_fusion.30
  327.6 3.0 multiply_reduce_fusion.15
  332.5 2.4 copy.396
  334.9 2.7 fusion.73
  337.7 2.9 convolution_convert_fusion.2
  341.3 3.4 convolution_convert_fusion.3
  345.9 5.0 convolution_convert_fusion
  351.6 5.5 all-gather.11
  360.8 4.9 fusion.90
  369.6 2.6 convolution_bitcast_fusion.3
  374.0 3.7 while.39
  377.7 3.0 multiply_reduce_fusion.20
  380.9 4.3 fusion.63
  385.2 2.3 copy.402
  387.5 2.7 fusion.84
  402.9 4.1 convolution_convert_fusion.1
  409.3 20.1 %reduce-scatter.9.cloned.1.call-done = bf16[384,768]{1,0:T(8,128)(2,1)} async-done(((bf16[1536,768]{1,0:T(8,128)(2,1)}), bf16[384,768]{1,0:T(8,128)(2,1)}) %reduce-scatter.9.cloned.1.call-update) | async-done | bytes 589840 | tf_op jit(solution)/shard_map/reduce_scatter | solution.py:248
  431.6 52.8 %reduce-scatter.7.cloned.1.call-done = bf16[192,3352]{1,0:T(8,128)(2,1)} async-done(((bf16[768,3352]{1,0:T(8,128)(2,1)}), bf16[192,3352]{1,0:T(8,128)(2,1)}) %reduce-scatter.7.cloned.1.call-update) | async-done | bytes 1287184 | tf_op jit(solution)/shard_map/reduce_scatter | solution.py:314
  484.4 3.0 bitcast_convert_fusion.2
  487.4 51.2 %reduce-scatter.5.cloned.1.call-done = bf16[192,3352]{1,0:T(8,128)(2,1)} async-done(((bf16[768,3352]{1,0:T(8,128)(2,1)}), bf16[192,3352]{1,0:T(8,128)(2,1)}) %reduce-scatter.5.cloned.1.call-update) | async-done | bytes 1287184 | tf_op jit(solution)/shard_map/reduce_scatter | solution.py:314
  538.6 3.1 bitcast_convert_fusion.3
  542.8 3.0 fusion.80
  550.0 4.7 fusion.136
  556.2 236.5 %all-reduce.33.cloned.1.call-done = (f32[1,192,3352]{2,1,0:T(8,128)}, f32[1,192,3352]{2,1,0:T(8,128)}, f32[1,384,768]{2,1,0:T(8,128)}, f32[1,384,768]{2,1,0:T(8,128)}) async-done(((f32[1,192,3352]{2,1,0:T(8,128)}, f32[1,192,3352]{2,1,0:T(8,128)}, f32[1,384,768]{2,1,0:T(8,128)}, f32[1,384,768]{2,1,0:T(8,128)}), (f32[1,192,3352]{2,1,0:T(8,128)}, f32[1,192,3352]{2,1,0:T(8,128)}, f32[1,384,768]{2,1,0:T(8,128)}, ...) | async-done | bytes 7507984 | tf_op jit(solution)/shard_map/psum | solution.py:339
  792.7 5.4 pad_maximum_fusion
  799.6 128.6 %all-reduce.31.cloned.1.call-done = (f32[2,768]{1,0:T(2,128)}, f32[2,4,1792]{2,1,0:T(4,128)}, f32[2,1792]{1,0:T(2,128)}, f32[2,24]{1,0:T(2,128)}, f32[2,24]{1,0:...) async-done(((f32[2,768]{1,0:T(2,128)}, f32[2,4,1792]{2,1,0:T(4,128)}, f32[2,1792]{1,0:T(2,128)}, f32[2,24]{1,0:T(2,128)}, f32[2,24]{1,0:T(2,128)}, ...) | async-done | bytes 90704 | tf_op jit(solution)/shard_map/psum | solution.py:347
  (584 shorter events, 157.9 us)
Async XLA Ops:
  7.2 4.8 copy-start.117
  7.2 45.6 %all-gather.21.cloned.1.call-start = ((), (), s32[]{:S(2)}) async-start(), calls=%async_computation.8 | async-start | bytes 6635520 | tf_op jit(solution)/shard_map/all_gather | solution.py:194
  10.7 87.7 %all-gather.23.cloned.1.call-start = ((), (), s32[]{:S(2)}) async-start(), calls=%async_computation.9 | async-start | bytes 3932160 | tf_op jit(solution)/shard_map/all_gather | solution.py:24
  11.4 44.9 %copy-start.90 = (f32[768]{0:T(1024)}, f32[768]{0:T(1024)S(1)}, u32[]{:S(2)}) copy-start(f32[768]{0:T(1024)S(1)} %get-tuple-element.724) | copy-start | bytes 9220
  12.7 48.4 %copy-start.103 = (f32[1792]{0:T(1024)}, f32[1792]{0:T(1024)S(1)}, u32[]{:S(2)}) copy-start(f32[1792]{0:T(1024)S(1)} %get-tuple-element.713) | copy-start | bytes 21508
  12.7 48.4 %copy-start.105 = (f32[1792]{0:T(1024)}, f32[1792]{0:T(1024)S(1)}, u32[]{:S(2)}) copy-start(f32[1792]{0:T(1024)S(1)} %get-tuple-element.714) | copy-start | bytes 21508
  12.7 48.4 %copy-start.107 = (f32[1792]{0:T(1024)}, f32[1792]{0:T(1024)S(1)}, u32[]{:S(2)}) copy-start(f32[1792]{0:T(1024)S(1)} %get-tuple-element.715) | copy-start | bytes 21508
  13.4 42.8 %copy-start.144 = (f32[128]{0:T(128)}, f32[128]{0:T(128)S(1)}, u32[]{:S(2)}) copy-start(f32[128]{0:T(128)S(1)} %fusion.199) | copy-start | bytes 1540
  13.9 42.3 %copy-start.154 = (f32[24]{0:T(128)}, f32[24]{0:T(128)S(1)}, u32[]{:S(2)}) copy-start(f32[24]{0:T(128)S(1)} %get-tuple-element.833) | copy-start | bytes 292
  13.9 43.2 %copy-start.134 = (f32[24]{0:T(128)}, f32[24]{0:T(128)S(1)}, u32[]{:S(2)}) copy-start(f32[24]{0:T(128)S(1)} %get-tuple-element.844) | copy-start | bytes 292
  56.3 4.6 copy-start.41
  56.5 16.4 %copy-start.54 = (f32[1,128,24]{2,1,0:T(8,128)}, f32[1,128,24]{2,1,0:T(8,128)S(1)}, u32[]{:S(2)}) copy-start(f32[1,128,24]{2,1,0:T(8,128)S(1)} %reduce_window_sum.47) | copy-start | bytes 36868
  57.8 3.1 collective-permute-start
  63.4 45.1 %copy-start.25 = (f32[128,1792]{1,0:T(8,128)}, f32[128,1792]{1,0:T(8,128)S(1)}, u32[]{:S(2)}) copy-start(f32[128,1792]{1,0:T(8,128)S(1)} %get-tuple-element.792) | copy-start | bytes 2752516
  68.0 56.1 %all-gather.25.cloned.1.call-start = ((), (), s32[]{:S(2)}) async-start(), calls=%async_computation.10 | async-start | bytes 2949120 | tf_op jit(solution)/shard_map/all_gather | solution.py:231
  70.4 96.4 %all-gather.27.cloned.1.call-start = ((), (), s32[]{:S(2)}) async-start(), calls=%async_computation.11 | async-start | bytes 6635520 | tf_op jit(solution)/shard_map/all_gather | solution.py:194
  71.0 143.9 %all-gather.29.cloned.1.call-start = ((), (), s32[]{:S(2)}) async-start(), calls=%async_computation.12 | async-start | bytes 3932160 | tf_op jit(solution)/shard_map/all_gather | solution.py:24
  81.0 28.3 %copy-start.18 = (f32[128,1536]{0,1:T(8,128)}, f32[128,1536]{0,1:T(8,128)S(1)}, u32[]{:S(2)}) copy-start(f32[128,1536]{0,1:T(8,128)S(1)} %copy.347) | copy-start | bytes 2359300
  81.3 28.0 %copy-start.66 = (f32[128,128]{1,0:T(8,128)}, f32[128,128]{1,0:T(8,128)S(1)}, u32[]{:S(2)}) copy-start(f32[128,128]{1,0:T(8,128)S(1)} %fusion.191) | copy-start | bytes 196612
  113.5 10.5 %copy-start.45 = (bf16[128,768]{1,0:T(8,128)(2,1)S(1)}, bf16[128,768]{1,0:T(8,128)(2,1)}, u32[]{:S(2)}) copy-start(bf16[128,768]{1,0:T(8,128)(2,1)} %param.24) | copy-start | bytes 589828
  115.0 9.0 copy-start.34
  116.7 9.7 %copy-start.4 = (f32[128,1536]{1,0:T(8,128)}, f32[128,1536]{1,0:T(8,128)S(1)}, u32[]{:S(2)}) copy-start(f32[128,1536]{1,0:T(8,128)S(1)} %get-tuple-element.791) | copy-start | bytes 2359300
  124.0 42.8 %copy-start.87 = (f32[768]{0:T(1024)S(1)}, f32[768]{0:T(1024)}, u32[]{:S(2)}) copy-start(f32[768]{0:T(1024)} %get-tuple-element.723) | copy-start | bytes 9220
  126.4 40.5 %copy-start.179 = (f32[128]{0:T(128)}, f32[128]{0:T(128)S(1)}, u32[]{:S(2)}) copy-start(f32[128]{0:T(128)S(1)} %get-tuple-element.834) | copy-start | bytes 1540
  126.4 43.9 %copy-start.20 = (f32[128,768]{1,0:T(8,128)}, f32[128,768]{1,0:T(8,128)S(1)}, u32[]{:S(2)}) copy-start(f32[128,768]{1,0:T(8,128)S(1)} %get-tuple-element.835) | copy-start | bytes 1179652
  126.4 43.9 %copy-start.146 = (f32[128]{0:T(128)}, f32[128]{0:T(128)S(1)}, u32[]{:S(2)}) copy-start(f32[128]{0:T(128)S(1)} %fusion.201) | copy-start | bytes 1540
  171.5 5.4 copy-start.56
  174.1 4.2 collective-permute-start.1
  185.4 55.0 %all-gather.31.cloned.1.call-start = ((), (), s32[]{:S(2)}) async-start(), calls=%async_computation.13 | async-start | bytes 2949120 | tf_op jit(solution)/shard_map/all_gather | solution.py:231
  186.0 98.8 %all-gather.33.cloned.1.call-start = ((), (), s32[]{:S(2)}) async-start(), calls=%async_computation.14 | async-start | bytes 1966080 | tf_op jit(solution)/shard_map/all_gather | solution.py:44
  225.1 55.5 %copy-start = (f32[24,64,128]{2,1,0:T(8,128)}, f32[24,64,128]{2,1,0:T(8,128)S(1)}, u32[]{:S(2)}) copy-start(f32[24,64,128]{2,1,0:T(8,128)S(1)} %get-tuple-element.636) | copy-start | bytes 2359300
  253.0 120.9 %all-gather.35.cloned.1.call-start = ((), (), s32[]{:S(2)}) async-start(), calls=%async_computation.15 | async-start | bytes 1966080 | tf_op jit(solution)/shard_map/all_gather | solution.py:44
  306.8 6.7 copy-start.76
  306.8 6.7 copy-start.157
  308.4 8.1 collective-permute-start.2
  319.7 5.2 copy-start.180
  319.7 5.2 copy-start.22
  319.7 5.2 copy-start.61
  319.7 5.2 copy-start.88
  319.7 5.2 copy-start.147
  319.7 5.4 copy-start.29
  319.7 5.4 copy-start.85
  319.7 5.4 copy-start.149
  332.5 5.2 copy-start.3
  332.5 5.2 copy-start.62
  337.6 69.5 %reduce-scatter.11.cloned.1.call-start = ((), (), s32[]{:S(2)}) async-start(), calls=%async_computation.7 | async-start | bytes 2949120 | tf_op jit(solution)/shard_map/reduce_scatter | solution.py:248
  340.6 88.8 %reduce-scatter.9.cloned.1.call-start = ((), (), s32[]{:S(2)}) async-start(), calls=%async_computation.6 | async-start | bytes 2949120 | tf_op jit(solution)/shard_map/reduce_scatter | solution.py:248
  344.7 139.6 %reduce-scatter.7.cloned.1.call-start = ((), (), s32[]{:S(2)}) async-start(), calls=%async_computation.5 | async-start | bytes 6635520 | tf_op jit(solution)/shard_map/reduce_scatter | solution.py:314
  351.0 187.6 %reduce-scatter.5.cloned.1.call-start = ((), (), s32[]{:S(2)}) async-start(), calls=%async_computation.4 | async-start | bytes 6635520 | tf_op jit(solution)/shard_map/reduce_scatter | solution.py:314
  358.5 7.2 copy-start.16
  385.2 5.0 copy-start.74
  393.6 8.2 collective-permute-start.3
  407.0 385.6 %all-reduce.33.cloned.1.call-start = ((), (), s32[]{:S(2)}) async-start(), calls=%async_computation.17 | async-start | bytes 15335424 | tf_op jit(solution)/shard_map/psum | solution.py:339
  541.7 386.5 %all-reduce.31.cloned.1.call-start = ((), (), s32[]{:S(2)}) async-start(), calls=%async_computation.16 | async-start | bytes 186368 | tf_op jit(solution)/shard_map/psum | solution.py:347
  542.8 4.7 copy-start.130
  542.8 4.7 copy-start.129
  542.8 4.7 copy-start.128
  542.8 4.7 copy-start.170
  542.8 5.3 copy-start.164
  542.8 5.3 copy-start.169
  550.0 5.3 copy-start.176
  550.0 5.3 copy-start.40
  792.7 5.4 copy-start.64
  792.7 5.4 copy-start.65
  (138 other events, 313.7 us)
Sparse Core Ops, SparseCore 0:
  10.8 41.9 all-gather.20
  68.1 30.2 all-gather.22
  100.0 24.0 all-gather.24
  126.0 40.7 all-gather.26
  185.5 29.3 all-gather.28
  216.3 24.0 all-gather.30
  253.1 19.6 all-gather.32
  337.8 20.4 all-gather.34
  361.3 32.8 reduce-scatter.10
  396.6 32.8 reduce-scatter.8
  432.5 51.7 reduce-scatter.6
  486.8 51.7 reduce-scatter.4
  544.3 248.2 all-reduce.32
  800.1 128.0 all-reduce.30
where the time goes:
time: 956 us; the launch traced here: 944 us
  waiting for transfers between devices  607 us (63%)
  matrix products  106 us (11%)
  local copies, waits for them, and re-layouts  92.1 us (10%)
  other arithmetic  91.7 us (10%)
  blocking collectives  22.1 us (2%)
  between operations  16.5 us (2%)
    psum x1, waiting for transfers between devices, shards(): grad_in_w, grad_out_w = lax.psum((grad_in_w, grad_out_w), 'replica')  236 us
    psum x1, waiting for transfers between devices, shards(): lax.psum((columns[0], columns[1], columns[2], columns[3], columns[4], col...  129 us
    reduce_scatter x2, waiting for transfers between devices, shards(): lax.psum_scatter(in_term(jnp.int32(0), lax.axis_size('shard') * in_rows)....  104 us
    all_gather x2, waiting for transfers between devices, shards(): lax.all_gather(in_weight[section_no], 'shard', axis=0, tiled=True)  79.3 us
    all_gather x2, waiting for transfers between devices, carried_in(): everything = jax.tree.map(lambda part: lax.all_gather(part, axis), array)  27.5 us
    dot_general x6, matrix products, outputs(): inside = jnp.einsum('chts,cshp->cthp', mixing, x_heads, precision=EXACT)  25.9 us
    unnamed x375, local copies, waits for them, and re-layouts  22.9 us
    reduce_scatter x2, waiting for transfers between devices, shards(): lax.psum_scatter(out_term(jnp.int32(0), lax.axis_size('shard') * out_rows...  20.1 us
  transfers between devices with their start and end apart: 18, of which 11 were waited for; matrix products, arithmetic and copies ran while one was open for 20% of the time, Pallas kernels for 0%

commit v1 on v0

--- a/solution.py
+++ b/solution.py
@@ -345,8 +345,11 @@
         jnp.stack([small[number][member] for number in range(layer_count)]) for member in range(7)
     ]
     summed = lax.psum(
-        (columns[0], columns[1], columns[2], columns[3], columns[4], columns[5], columns[6]),
-        ("replica", "shard"),
+        lax.psum(
+            (columns[0], columns[1], columns[2], columns[3], columns[4], columns[5], columns[6]),
+            "shard",
+        ),
+        "replica",
     )
     return (
         block_out,

time: 956 us -> 935 us (0.978)
  waiting for transfers between devices: 607 us -> 583 us
    psum x1, waiting for transfers between devices: 129 us -> 28.4 us  [shards(): lax.psum((columns[0], columns[1], columns[2], columns[3], columns[4], col...]
    psum x0 -> x1, waiting for transfers between devices: none -> 69.2 us  [shards(): lax.psum(lax.psum((columns[0], columns[1], columns[2], columns[3], column...]
    psum x1, waiting for transfers between devices: 236 us -> 254 us  [shards(): grad_in_w, grad_out_w = lax.psum((grad_in_w, grad_out_w), 'replica')]
    reduce_scatter x2, waiting for transfers between devices: 20.1 us -> 10.2 us  [shards(): lax.psum_scatter(out_term(jnp.int32(0), lax.axis_size('shard') * out_rows...]
  transfers between devices with their start and end apart: 18 -> 19, of which waited for: 11 -> 12; matrix products, arithmetic and copies ran while one was open for 20% -> 20% of each run, Pallas kernels for 0% -> 0%
where the time goes in v1:
time: 935 us; the launch traced here: 921 us
  waiting for transfers between devices  583 us (62%)
  matrix products  106 us (11%)
  local copies, waits for them, and re-layouts  92.6 us (10%)
  other arithmetic  91.9 us (10%)
  blocking collectives  22.4 us (2%)
  between operations  16.6 us (2%)
    psum x1, waiting for transfers between devices, shards(): grad_in_w, grad_out_w = lax.psum((grad_in_w, grad_out_w), 'replica')  254 us
    reduce_scatter x2, waiting for transfers between devices, shards(): lax.psum_scatter(in_term(jnp.int32(0), lax.axis_size('shard') * in_rows)....  104 us
    all_gather x2, waiting for transfers between devices, shards(): lax.all_gather(in_weight[section_no], 'shard', axis=0, tiled=True)  79.2 us
    psum x1, waiting for transfers between devices, shards(): lax.psum(lax.psum((columns[0], columns[1], columns[2], columns[3], column...  69.2 us
    psum x1, waiting for transfers between devices, shards(): lax.psum((columns[0], columns[1], columns[2], columns[3], columns[4], col...  28.4 us
    all_gather x2, waiting for transfers between devices, carried_in(): everything = jax.tree.map(lambda part: lax.all_gather(part, axis), array)  27 us
    dot_general x6, matrix products, outputs(): inside = jnp.einsum('chts,cshp->cthp', mixing, x_heads, precision=EXACT)  26 us
    unnamed x375, local copies, waits for them, and re-layouts  23.5 us
  transfers between devices with their start and end apart: 19, of which 12 were waited for; matrix products, arithmetic and copies ran while one was open for 20% of the time, Pallas kernels for 0%

profile of v1, /device:TPU:8, one launch (start us, length us, event | category | flops | bytes accessed | tf_op | source)
XLA Modules:
  0.0 920.8 jit_solution(5300321304736337917)
XLA Ops:
  7.3 3.4 fusion.225
  13.9 38.8 %all-gather.21.cloned.1.call-done = bf16[1,768,3352]{2,1,0:T(8,128)(2,1)} async-done(((bf16[1,192,3352]{2,1,0:T(8,128)(2,1)}), bf16[1,768,3352]{2,1,0:T(8,128)(2,1)}) %all-gather.21.cloned.1.call-update) | async-done | bytes 5148688 | tf_op jit(solution)/shard_map/all_gather | solution.py:194
  52.8 3.4 fusion.10
  68.1 2.3 fusion.226
  74.4 5.3 all-gather.2
  81.4 17.1 %all-gather.23.cloned.1.call-done = f32[96,64,128]{2,1,0:T(8,128)} async-done(((f32[24,64,128]{2,1,0:T(8,128)}), f32[96,64,128]{2,1,0:T(8,128)}) %all-gather.23.cloned.1.call-update) | async-done | bytes 3145744 | tf_op jit(solution)/shard_map/all_gather | solution.py:24
  98.4 10.1 %while.40 = (s32[]{:T(128)}, f32[24,64,128]{2,1,0:T(8,128)S(1)}, s32[]{:T(128)}, f32[4,24,64,128]{3,2,1,0:T(8,128)}, f32[4,24]{1,0:T(4,128)}, /*index=5*/s32[]{:T(128)}, s32[]{:T(128)}) while((s32[]{:T(128)}, f32[24,64,128]{2,1,0:T(8,128)S(1)}, s32[]{:T(128)}, f32[4,24,64,128]{3,2,1,0:T(8,128)}, f32[4,24]{1,0:T(4,128)}, ...), condition=%wide.region_3.4_spmd.clone, body=%wide.region_2.3_spmd.clone.sunk | while | flops 786436 | bytes 2359697 | solution.py:36
  109.5 4.1 fusion.69
  117.9 6.2 all-gather.25.cloned.1.call-done
  124.1 2.3 multiply_reduce_fusion.32
  126.5 40.4 %all-gather.27.cloned.1.call-done = bf16[1,768,3352]{2,1,0:T(8,128)(2,1)} async-done(((bf16[1,192,3352]{2,1,0:T(8,128)(2,1)}), bf16[1,768,3352]{2,1,0:T(8,128)(2,1)}) %all-gather.27.cloned.1.call-update) | async-done | bytes 5148688 | tf_op jit(solution)/shard_map/all_gather | solution.py:194
  166.9 3.5 fusion.13
  174.1 2.4 collective-permute-start.1
  182.9 2.6 convolution_add_fusion.2
  192.3 2.4 copy.374
  194.7 6.2 all-gather.6
  200.9 2.3 copy.358
  205.0 9.9 %all-gather.29.cloned.1.call-done = f32[96,64,128]{2,1,0:T(8,128)} async-done(((f32[24,64,128]{2,1,0:T(8,128)}), f32[96,64,128]{2,1,0:T(8,128)}) %all-gather.29.cloned.1.call-update) | async-done | bytes 3145744 | tf_op jit(solution)/shard_map/all_gather | solution.py:24
  214.9 10.1 %while.41 = (s32[]{:T(128)}, f32[24,64,128]{2,1,0:T(8,128)S(1)}, s32[]{:T(128)}, f32[4,24,64,128]{3,2,1,0:T(8,128)}, f32[4,24]{1,0:T(4,128)}, /*index=5*/s32[]{:T(128)}, s32[]{:T(128)}) while((s32[]{:T(128)}, f32[24,64,128]{2,1,0:T(8,128)S(1)}, s32[]{:T(128)}, f32[4,24,64,128]{3,2,1,0:T(8,128)}, f32[4,24]{1,0:T(4,128)}, ...), condition=%wide.region_8.9_spmd.clone, body=%wide.region_7.8_spmd.clone.sunk | while | flops 786436 | bytes 2359697 | solution.py:36
  227.1 4.1 fusion.57
  231.2 2.3 copy.367
  233.5 2.4 multiply_reduce_fusion.28
  237.0 3.4 all-gather.31.cloned.1.call-done
  240.4 3.6 multiply_reduce_fusion.12
  248.0 2.3 copy.375
  250.2 2.7 fusion.72
  254.7 2.3 copy.395
  257.0 5.4 all-gather.9
  263.0 2.3 copy.376
  268.8 5.7 fusion.88
  280.6 2.5 convolution_bitcast_fusion.5
  284.9 6.2 while.38
  291.2 2.7 multiply_reduce_fusion.26
  294.8 2.8 fusion.51
  297.6 2.3 copy.381
  299.9 2.7 fusion.86
  302.6 2.3 multiply_reduce_fusion.7
  319.8 5.1 multiply_reduce_fusion.30
  327.6 3.1 multiply_reduce_fusion.15
  332.5 2.4 copy.396
  334.9 2.7 fusion.73
  337.7 2.9 convolution_convert_fusion.2
  341.3 3.4 convolution_convert_fusion.3
  345.9 5.0 convolution_convert_fusion
  351.6 5.4 all-gather.11
  360.8 4.9 fusion.90
  369.6 2.6 convolution_bitcast_fusion.3
  374.0 3.7 while.39
  377.8 3.0 multiply_reduce_fusion.20
  380.9 4.3 fusion.63
  385.2 2.3 copy.402
  387.6 2.7 fusion.84
  403.0 4.1 convolution_convert_fusion.1
  414.3 4.2 fusion.136
  419.2 10.2 %reduce-scatter.9.cloned.1.call-done = bf16[384,768]{1,0:T(8,128)(2,1)} async-done(((bf16[1536,768]{1,0:T(8,128)(2,1)}), bf16[384,768]{1,0:T(8,128)(2,1)}) %reduce-scatter.9.cloned.1.call-update) | async-done | bytes 589840 | tf_op jit(solution)/shard_map/reduce_scatter | solution.py:248
  431.6 52.8 %reduce-scatter.7.cloned.1.call-done = bf16[192,3352]{1,0:T(8,128)(2,1)} async-done(((bf16[768,3352]{1,0:T(8,128)(2,1)}), bf16[192,3352]{1,0:T(8,128)(2,1)}) %reduce-scatter.7.cloned.1.call-update) | async-done | bytes 1287184 | tf_op jit(solution)/shard_map/reduce_scatter | solution.py:314
  484.4 3.0 bitcast_convert_fusion.2
  487.4 51.2 %reduce-scatter.5.cloned.1.call-done = bf16[192,3352]{1,0:T(8,128)(2,1)} async-done(((bf16[768,3352]{1,0:T(8,128)(2,1)}), bf16[192,3352]{1,0:T(8,128)(2,1)}) %reduce-scatter.5.cloned.1.call-update) | async-done | bytes 1287184 | tf_op jit(solution)/shard_map/reduce_scatter | solution.py:314
  538.6 3.0 bitcast_convert_fusion.3
  542.6 2.9 fusion.80
  546.4 28.4 %all-reduce.37.cloned.1.call-done = (f32[2,768]{1,0:T(2,128)}, f32[2,4,1792]{2,1,0:T(4,128)}, f32[2,1792]{1,0:T(2,128)}, f32[2,24]{1,0:T(2,128)}, f32[2,24]{1,0:...) async-done(((f32[2,768]{1,0:T(2,128)}, f32[2,4,1792]{2,1,0:T(4,128)}, f32[2,1792]{1,0:T(2,128)}, f32[2,24]{1,0:T(2,128)}, f32[2,24]{1,0:T(2,128)}, ...) | async-done | bytes 90704 | tf_op jit(solution)/shard_map/psum | solution.py:348
  574.8 253.9 %all-reduce.35.cloned.1.call-done = (f32[1,192,3352]{2,1,0:T(8,128)}, f32[1,192,3352]{2,1,0:T(8,128)}, f32[1,384,768]{2,1,0:T(8,128)}, f32[1,384,768]{2,1,0:T(8,128)}) async-done(((f32[1,192,3352]{2,1,0:T(8,128)}, f32[1,192,3352]{2,1,0:T(8,128)}, f32[1,384,768]{2,1,0:T(8,128)}, f32[1,384,768]{2,1,0:T(8,128)}), (f32[1,192,3352]{2,1,0:T(8,128)}, f32[1,192,3352]{2,1,0:T(8,128)}, f32[1,384,768]{2,1,0:T(8,128)}, ...) | async-done | bytes 7507984 | tf_op jit(solution)/shard_map/psum | solution.py:339
  828.7 5.4 pad_maximum_fusion
  835.7 69.2 %all-reduce.33.cloned.1.call-done = (f32[2,768]{1,0:T(2,128)}, f32[2,4,1792]{2,1,0:T(4,128)}, f32[2,1792]{1,0:T(2,128)}, f32[2,24]{1,0:T(2,128)}, f32[2,24]{1,0:...) async-done(((f32[2,768]{1,0:T(2,128)}, f32[2,4,1792]{2,1,0:T(4,128)}, f32[2,1792]{1,0:T(2,128)}, f32[2,24]{1,0:T(2,128)}, f32[2,24]{1,0:T(2,128)}, ...) | async-done | bytes 90704 | tf_op jit(solution)/shard_map/psum | solution.py:347
  (587 shorter events, 160.8 us)
Async XLA Ops:
  7.2 4.8 copy-start.117
  7.2 45.6 %all-gather.21.cloned.1.call-start = ((), (), s32[]{:S(2)}) async-start(), calls=%async_computation.8 | async-start | bytes 6635520 | tf_op jit(solution)/shard_map/all_gather | solution.py:194
  10.7 87.7 %all-gather.23.cloned.1.call-start = ((), (), s32[]{:S(2)}) async-start(), calls=%async_computation.9 | async-start | bytes 3932160 | tf_op jit(solution)/shard_map/all_gather | solution.py:24
  11.4 44.9 %copy-start.90 = (f32[768]{0:T(1024)}, f32[768]{0:T(1024)S(1)}, u32[]{:S(2)}) copy-start(f32[768]{0:T(1024)S(1)} %get-tuple-element.724) | copy-start | bytes 9220
  12.7 48.6 %copy-start.103 = (f32[1792]{0:T(1024)}, f32[1792]{0:T(1024)S(1)}, u32[]{:S(2)}) copy-start(f32[1792]{0:T(1024)S(1)} %get-tuple-element.713) | copy-start | bytes 21508
  12.7 48.6 %copy-start.105 = (f32[1792]{0:T(1024)}, f32[1792]{0:T(1024)S(1)}, u32[]{:S(2)}) copy-start(f32[1792]{0:T(1024)S(1)} %get-tuple-element.714) | copy-start | bytes 21508
  12.7 48.6 %copy-start.107 = (f32[1792]{0:T(1024)}, f32[1792]{0:T(1024)S(1)}, u32[]{:S(2)}) copy-start(f32[1792]{0:T(1024)S(1)} %get-tuple-element.715) | copy-start | bytes 21508
  13.4 42.8 %copy-start.144 = (f32[128]{0:T(128)}, f32[128]{0:T(128)S(1)}, u32[]{:S(2)}) copy-start(f32[128]{0:T(128)S(1)} %fusion.199) | copy-start | bytes 1540
  13.9 42.3 %copy-start.154 = (f32[24]{0:T(128)}, f32[24]{0:T(128)S(1)}, u32[]{:S(2)}) copy-start(f32[24]{0:T(128)S(1)} %get-tuple-element.840) | copy-start | bytes 292
  13.9 43.2 %copy-start.134 = (f32[24]{0:T(128)}, f32[24]{0:T(128)S(1)}, u32[]{:S(2)}) copy-start(f32[24]{0:T(128)S(1)} %get-tuple-element.851) | copy-start | bytes 292
  56.3 4.8 copy-start.41
  56.5 16.5 %copy-start.54 = (f32[1,128,24]{2,1,0:T(8,128)}, f32[1,128,24]{2,1,0:T(8,128)S(1)}, u32[]{:S(2)}) copy-start(f32[1,128,24]{2,1,0:T(8,128)S(1)} %reduce_window_sum.47) | copy-start | bytes 36868
  57.8 3.2 collective-permute-start
  63.5 45.1 %copy-start.25 = (f32[128,1792]{1,0:T(8,128)}, f32[128,1792]{1,0:T(8,128)S(1)}, u32[]{:S(2)}) copy-start(f32[128,1792]{1,0:T(8,128)S(1)} %get-tuple-element.799) | copy-start | bytes 2752516
  68.1 56.0 %all-gather.25.cloned.1.call-start = ((), (), s32[]{:S(2)}) async-start(), calls=%async_computation.10 | async-start | bytes 2949120 | tf_op jit(solution)/shard_map/all_gather | solution.py:231
  70.5 96.4 %all-gather.27.cloned.1.call-start = ((), (), s32[]{:S(2)}) async-start(), calls=%async_computation.11 | async-start | bytes 6635520 | tf_op jit(solution)/shard_map/all_gather | solution.py:194
  71.1 143.8 %all-gather.29.cloned.1.call-start = ((), (), s32[]{:S(2)}) async-start(), calls=%async_computation.12 | async-start | bytes 3932160 | tf_op jit(solution)/shard_map/all_gather | solution.py:24
  81.1 28.3 %copy-start.18 = (f32[128,1536]{0,1:T(8,128)}, f32[128,1536]{0,1:T(8,128)S(1)}, u32[]{:S(2)}) copy-start(f32[128,1536]{0,1:T(8,128)S(1)} %copy.347) | copy-start | bytes 2359300
  81.3 28.1 %copy-start.66 = (f32[128,128]{1,0:T(8,128)}, f32[128,128]{1,0:T(8,128)S(1)}, u32[]{:S(2)}) copy-start(f32[128,128]{1,0:T(8,128)S(1)} %fusion.191) | copy-start | bytes 196612
  113.6 10.5 %copy-start.45 = (bf16[128,768]{1,0:T(8,128)(2,1)S(1)}, bf16[128,768]{1,0:T(8,128)(2,1)}, u32[]{:S(2)}) copy-start(bf16[128,768]{1,0:T(8,128)(2,1)} %param.24) | copy-start | bytes 589828
  115.1 9.0 copy-start.34
  116.7 9.7 %copy-start.4 = (f32[128,1536]{1,0:T(8,128)}, f32[128,1536]{1,0:T(8,128)S(1)}, u32[]{:S(2)}) copy-start(f32[128,1536]{1,0:T(8,128)S(1)} %get-tuple-element.798) | copy-start | bytes 2359300
  124.1 42.8 %copy-start.87 = (f32[768]{0:T(1024)S(1)}, f32[768]{0:T(1024)}, u32[]{:S(2)}) copy-start(f32[768]{0:T(1024)} %get-tuple-element.723) | copy-start | bytes 9220
  126.4 40.5 %copy-start.179 = (f32[128]{0:T(128)}, f32[128]{0:T(128)S(1)}, u32[]{:S(2)}) copy-start(f32[128]{0:T(128)S(1)} %get-tuple-element.841) | copy-start | bytes 1540
  126.4 43.9 %copy-start.20 = (f32[128,768]{1,0:T(8,128)}, f32[128,768]{1,0:T(8,128)S(1)}, u32[]{:S(2)}) copy-start(f32[128,768]{1,0:T(8,128)S(1)} %get-tuple-element.842) | copy-start | bytes 1179652
  126.5 43.9 %copy-start.146 = (f32[128]{0:T(128)}, f32[128]{0:T(128)S(1)}, u32[]{:S(2)}) copy-start(f32[128]{0:T(128)S(1)} %fusion.201) | copy-start | bytes 1540
  171.6 5.4 copy-start.56
  174.1 4.3 collective-permute-start.1
  185.5 54.9 %all-gather.31.cloned.1.call-start = ((), (), s32[]{:S(2)}) async-start(), calls=%async_computation.13 | async-start | bytes 2949120 | tf_op jit(solution)/shard_map/all_gather | solution.py:231
  186.1 98.8 %all-gather.33.cloned.1.call-start = ((), (), s32[]{:S(2)}) async-start(), calls=%async_computation.14 | async-start | bytes 1966080 | tf_op jit(solution)/shard_map/all_gather | solution.py:44
  225.0 55.7 %copy-start = (f32[24,64,128]{2,1,0:T(8,128)}, f32[24,64,128]{2,1,0:T(8,128)S(1)}, u32[]{:S(2)}) copy-start(f32[24,64,128]{2,1,0:T(8,128)S(1)} %get-tuple-element.636) | copy-start | bytes 2359300
  253.0 120.9 %all-gather.35.cloned.1.call-start = ((), (), s32[]{:S(2)}) async-start(), calls=%async_computation.15 | async-start | bytes 1966080 | tf_op jit(solution)/shard_map/all_gather | solution.py:44
  306.8 6.7 copy-start.76
  306.8 6.7 copy-start.157
  308.4 8.1 collective-permute-start.2
  319.7 5.2 copy-start.180
  319.7 5.2 copy-start.22
  319.7 5.2 copy-start.61
  319.7 5.2 copy-start.88
  319.7 5.2 copy-start.147
  319.7 5.4 copy-start.29
  319.7 5.4 copy-start.85
  319.7 5.4 copy-start.149
  332.5 5.2 copy-start.3
  332.5 5.2 copy-start.62
  337.6 71.9 %reduce-scatter.11.cloned.1.call-start = ((), (), s32[]{:S(2)}) async-start(), calls=%async_computation.7 | async-start | bytes 2949120 | tf_op jit(solution)/shard_map/reduce_scatter | solution.py:248
  340.6 88.8 %reduce-scatter.9.cloned.1.call-start = ((), (), s32[]{:S(2)}) async-start(), calls=%async_computation.6 | async-start | bytes 2949120 | tf_op jit(solution)/shard_map/reduce_scatter | solution.py:248
  344.7 139.6 %reduce-scatter.7.cloned.1.call-start = ((), (), s32[]{:S(2)}) async-start(), calls=%async_computation.5 | async-start | bytes 6635520 | tf_op jit(solution)/shard_map/reduce_scatter | solution.py:314
  351.0 187.6 %reduce-scatter.5.cloned.1.call-start = ((), (), s32[]{:S(2)}) async-start(), calls=%async_computation.4 | async-start | bytes 6635520 | tf_op jit(solution)/shard_map/reduce_scatter | solution.py:314
  358.5 7.2 copy-start.16
  385.2 5.0 copy-start.74
  393.7 8.2 collective-permute-start.3
  407.2 4.5 copy-start.131
  407.2 4.5 copy-start.130
  407.2 4.6 copy-start.129
  407.2 4.6 copy-start.128
  407.2 4.6 copy-start.170
  407.2 5.2 copy-start.164
  407.3 5.2 copy-start.169
  407.3 167.5 %all-reduce.37.cloned.1.call-start = ((), (), s32[]{:S(2)}) async-start(), calls=%async_computation.18 | async-start | bytes 186368 | tf_op jit(solution)/shard_map/psum | solution.py:348
  419.1 409.5 %all-reduce.35.cloned.1.call-start = ((), (), s32[]{:S(2)}) async-start(), calls=%async_computation.17 | async-start | bytes 15335424 | tf_op jit(solution)/shard_map/psum | solution.py:339
  541.6 363.2 %all-reduce.33.cloned.1.call-start = ((), (), s32[]{:S(2)}) async-start(), calls=%async_computation.16 | async-start | bytes 186368 | tf_op jit(solution)/shard_map/psum | solution.py:347
  828.7 5.4 copy-start.64
  828.7 5.4 copy-start.65
  (139 other events, 298.7 us)
Sparse Core Ops, SparseCore 0:
  10.8 41.9 all-gather.20
  68.2 30.1 all-gather.22
  100.0 24.0 all-gather.24
  126.1 40.7 all-gather.26
  185.6 29.2 all-gather.28
  216.3 24.0 all-gather.30
  253.1 19.6 all-gather.32
  337.8 20.4 all-gather.34
  361.3 32.8 reduce-scatter.10
  396.6 32.8 reduce-scatter.8
  432.5 51.7 reduce-scatter.6
  486.8 51.7 reduce-scatter.4
  542.6 32.1 all-reduce.36
  580.4 248.2 all-reduce.34
  832.7 72.0 all-reduce.32
